TPU v7x, 512 devices: a whole 4x4x16 slice. The times are simulated.
512 devices in a mesh: expert: 128 (over y, x, z_lo), hidden: 4 (over z_hi, core).
Axes of the slice: x: 4, y: 4, z: 16 (z_hi: 2, z_lo: 8; z = z_hi * 8 + z_lo), core: 2. Of those that a mesh axis runs over, the one named last changes fastest.
Arguments:
- tokens: bfloat16 [256, 196, 1024], P('expert', None, 'hidden'), may hold values from -64 to 64
- slot_params: bfloat16 [1024, 128], P('hidden'), may hold values from -0.4 to 0.4
- weight_in: bfloat16 [128, 1024, 4096], P('expert', None, 'hidden'), may hold values from -0.1875 to 0.1875
- bias_in: bfloat16 [128, 4096], P('expert', 'hidden'), may hold values from -3 to 3
- weight_out: bfloat16 [128, 4096, 1024], P('expert', 'hidden'), may hold values from -0.09375 to 0.09375
- bias_out: bfloat16 [128, 1024], P('expert', 'hidden'), may hold values from -3 to 3
- cotangent: bfloat16 [256, 196, 1024], P('expert', None, 'hidden'), may hold values from -1.5 to 1.5
Outputs:
- mixed: bfloat16 [256, 196, 1024], P('expert', None, 'hidden')
- token_grad: bfloat16 [256, 196, 1024], P('expert', None, 'hidden')
- zloss: float32 [256, 196], P('expert')
All inputs are finite; a program needn't handle non-finite values.
Results may differ from a plain program's by a relative error of at most 0.015.
Values may be sent and summed in bfloat16 or wider, within the bound.
A program may use at most 64 MiB of HBM per device.

v0:
```python
import jax
import jax.numpy as jnp
from jax import lax
from jax.sharding import PartitionSpec as P

loss_weight = 0.1


def sent_to_all(x, axis):
    copies = jnp.broadcast_to(x, (lax.axis_size(axis), *x.shape))
    return lax.all_to_all(copies, axis, split_axis=0, concat_axis=0, tiled=True)


def of_everyone(x, axis):
    everything = sent_to_all(x, axis)
    return jnp.sum(everything, axis=0)


def in_order(tiles, dim):
    tiles = jnp.moveaxis(tiles, 0, dim)
    lengths = tiles.shape
    return tiles.reshape(*lengths[:dim], lengths[dim] * lengths[dim + 1], *lengths[dim + 2 :])


def gathered_copies(x, axis, dim):
    return in_order(sent_to_all(x, axis), dim)


def split_up(x, dim, peers):
    lengths = x.shape
    tiles = x.reshape(*lengths[:dim], peers, lengths[dim] // peers, *lengths[dim + 1 :])
    return jnp.moveaxis(tiles, dim, 0)


def sent_and_summed(x, axis, dim):
    peers = lax.axis_size(axis)
    tiles = lax.all_to_all(split_up(x, dim, peers), axis, 0, 0, tiled=True)
    return jnp.sum(tiles.astype(jnp.float32), axis=0)


def taken_together(x, axis):
    everything = sent_to_all(x, axis)
    return jnp.sum(everything.astype(jnp.float32), axis=0)


def gelu_parts(value):
    factor = 0.7978845608028654
    inner = factor * (value + 0.044715 * value * value * value)
    slope_tanh = jnp.tanh(inner)
    result = 0.5 * value * (1.0 + slope_tanh)
    slope = 0.5 * (1.0 + slope_tanh) + 0.5 * value * (1.0 - slope_tanh * slope_tanh) * factor * (
        1.0 + 3.0 * 0.044715 * value * value
    )
    return (result, slope)


def per_device(tokens, slot_params, weight_in, bias_in, weight_out, bias_out, cotangent):
    images_dev = tokens.shape[0]
    groups = lax.axis_size("expert")
    local_experts = weight_in.shape[0]
    quarter = tokens.shape[2]
    partial_value = jnp.einsum(
        "itd,ds->its", tokens, slot_params, preferred_element_type=jnp.float32
    )
    logits = of_everyone(partial_value, "hidden")
    dispatch = jax.nn.softmax(logits, axis=1)
    combine = jax.nn.softmax(logits, axis=2)
    log_total = jax.nn.logsumexp(logits, axis=2)
    zloss = loss_weight * log_total * log_total
    dispatch_low = dispatch.astype(jnp.bfloat16)
    combine_low = combine.astype(jnp.bfloat16)
    slot_in = jnp.einsum(
        "its,itd->isd", dispatch_low, tokens, preferred_element_type=jnp.float32
    ).astype(jnp.bfloat16)
    arrived = lax.all_to_all(slot_in, "expert", split_axis=1, concat_axis=0, tiled=True)
    pre_act = jnp.einsum(
        "ren,enf->ref",
        gathered_copies(arrived, "hidden", 2),
        weight_in,
        preferred_element_type=jnp.float32,
    )
    pre_act = pre_act + bias_in.astype(jnp.float32)[None]
    activated, slope = gelu_parts(pre_act)
    act_low = activated.astype(jnp.bfloat16)
    out_terms = jnp.einsum("ref,efd->red", act_low, weight_out, preferred_element_type=jnp.float32)
    expert_out = sent_and_summed(out_terms.astype(jnp.bfloat16), "hidden", 2)
    expert_low = (expert_out + bias_out.astype(jnp.float32)[None]).astype(jnp.bfloat16)
    slot_out = lax.all_to_all(
        expert_low.reshape(groups, images_dev, local_experts, quarter),
        "expert",
        split_axis=0,
        concat_axis=2,
        tiled=True,
    )
    slot_out = slot_out.reshape(images_dev, groups * local_experts, quarter)
    mixed = jnp.einsum(
        "its,isd->itd", combine_low, slot_out, preferred_element_type=jnp.float32
    ).astype(jnp.bfloat16)
    combine_part = jnp.einsum(
        "itd,isd->its", cotangent, slot_out, preferred_element_type=jnp.float32
    )
    out_grad = jnp.einsum(
        "its,itd->isd", combine_low, cotangent, preferred_element_type=jnp.float32
    ).astype(jnp.bfloat16)
    grad_arrived = lax.all_to_all(out_grad, "expert", split_axis=1, concat_axis=0, tiled=True)
    hidden_grad = jnp.einsum(
        "ren,efn->ref",
        gathered_copies(grad_arrived, "hidden", 2),
        weight_out,
        preferred_element_type=jnp.float32,
    )
    pre_grad = (hidden_grad * slope).astype(jnp.bfloat16)
    in_terms = jnp.einsum("ref,ekf->rek", pre_grad, weight_in, preferred_element_type=jnp.float32)
    slot_grad = sent_and_summed(in_terms.astype(jnp.bfloat16), "hidden", 2).astype(jnp.bfloat16)
    in_grad = lax.all_to_all(
        slot_grad.reshape(groups, images_dev, local_experts, quarter),
        "expert",
        split_axis=0,
        concat_axis=2,
        tiled=True,
    )
    in_grad = in_grad.reshape(images_dev, groups * local_experts, quarter)
    dispatch_part = jnp.einsum("itd,isd->its", tokens, in_grad, preferred_element_type=jnp.float32)
    combine_grad, dispatch_grad = (
        taken_together(combine_part.astype(jnp.bfloat16), "hidden").astype(jnp.float32),
        taken_together(dispatch_part.astype(jnp.bfloat16), "hidden").astype(jnp.float32),
    )
    from_combine = (
        combine * (combine_grad - jnp.sum(combine * combine_grad, axis=2, keepdims=True))
        + 2.0 * loss_weight * log_total[:, :, None] * combine
    )
    from_dispatch = dispatch * (
        dispatch_grad - jnp.sum(dispatch * dispatch_grad, axis=1, keepdims=True)
    )
    logit_low = (from_combine + from_dispatch).astype(jnp.bfloat16)
    token_grad = jnp.einsum(
        "its,ds->itd", logit_low, slot_params, preferred_element_type=jnp.float32
    )
    token_grad = token_grad + jnp.einsum(
        "its,isd->itd", dispatch_low, in_grad, preferred_element_type=jnp.float32
    )
    return (mixed, token_grad.astype(jnp.bfloat16), zloss)


def solution(mesh):
    return jax.shard_map(
        per_device,
        mesh=mesh,
        in_specs=(
            P("expert", None, "hidden"),
            P("hidden", None),
            P("expert", None, "hidden"),
            P("expert", "hidden"),
            P("expert", "hidden", None),
            P("expert", "hidden"),
            P("expert", None, "hidden"),
        ),
        out_specs=(P("expert", None, "hidden"), P("expert", None, "hidden"), P("expert", None)),
        check_vma=False,
    )
```

profile of v0, /device:TPU:49, one launch (start us, length us, event | category | flops | bytes accessed | tf_op | source)
XLA Modules:
  0.0 364.0 jit_solution(17710383384347243278)
XLA Ops:
  0.6 1.3 fusion.66
  2.3 60.5 %all_to_all.101 = f32[4,2,196,128]{3,1,2,0:T(2,128)S(1)} all-to-all(f32[4,2,196,128]{3,1,2,0:T(2,128)S(1)} %broadcast_in_dim.12), channel_id=1, replica_groups=mesh['expert'=128,'hidden'=4] {'hidden'}, dimensions={0} | all-to-all | bytes 1605632 | tf_op jit(solution)/shard_map/all_to_all | solution.py:11
  64.4 1.2 fusion.99
  65.6 1.2 convolution_convert_fusion.2
  67.6 11.5 %all-to-all-start.1 = ((bf16[2,128,256]{2,0,1:T(2,128)(2,1)}), bf16[2,128,256]{2,0,1:T(2,128)(2,1)S(1)}, u32[]{:S(2)}, u32[]{:S(2)}) async-start(bf16[2,128,256]{2,0,1:T(2,128)(2,1)} %copy.114), calls=%async_computation.1 | async-start | bytes 262144 | tf_op jit(solution)/shard_map/all_to_all | solution.py:75
  80.1 10.7 %all-to-all-done.1 = bf16[2,128,256]{2,0,1:T(2,128)(2,1)S(1)} async-done(((bf16[2,128,256]{2,0,1:T(2,128)(2,1)}), bf16[2,128,256]{2,0,1:T(2,128)(2,1)S(1)}, u32[]{:S(2)}, u32[]{:S(2)}) %all-to-all-start.1) | async-done | bytes 131104 | tf_op jit(solution)/shard_map/all_to_all | solution.py:75
  90.8 11.6 %all-to-all-start.6 = ((bf16[2,128,256]{2,0,1:T(2,128)(2,1)}), bf16[2,128,256]{2,0,1:T(2,128)(2,1)S(1)}, u32[]{:S(2)}, u32[]{:S(2)}) async-start(bf16[2,128,256]{2,0,1:T(2,128)(2,1)} %copy.126), calls=%async_computation.6 | async-start | bytes 262144 | tf_op jit(solution)/shard_map/all_to_all | solution.py:105
  102.5 11.5 %all-to-all-done.6 = bf16[2,128,256]{2,0,1:T(2,128)(2,1)S(1)} async-done(((bf16[2,128,256]{2,0,1:T(2,128)(2,1)}), bf16[2,128,256]{2,0,1:T(2,128)(2,1)S(1)}, u32[]{:S(2)}, u32[]{:S(2)}) %all-to-all-start.6) | async-done | bytes 131104 | tf_op jit(solution)/shard_map/all_to_all | solution.py:105
  114.9 6.3 %all-to-all-start.2 = ((bf16[4,256,1,256]{1,3,2,0:T(8,128)(2,1)}), bf16[4,256,1,256]{1,3,2,0:T(8,128)(2,1)S(1)}, u32[]{:S(2)}, u32[]{:S(2)}) async-start(bf16[4,256,1,256]{1,3,2,0:T(8,128)(2,1)} %broadcast_in_dim.13), calls=%async_computation.2 | async-start | bytes 1048576 | tf_op jit(solution)/shard_map/all_to_all | solution.py:11
  121.4 33.5 %all-to-all-done.2 = bf16[4,256,1,256]{1,3,2,0:T(8,128)(2,1)S(1)} async-done(((bf16[4,256,1,256]{1,3,2,0:T(8,128)(2,1)}), bf16[4,256,1,256]{1,3,2,0:T(8,128)(2,1)S(1)}, u32[]{:S(2)}, u32[]{:S(2)}) %all-to-all-start.2) | async-done | bytes 524320 | tf_op jit(solution)/shard_map/all_to_all | solution.py:11
  155.7 4.0 %all-to-all-start.7 = ((bf16[4,256,1,256]{1,3,2,0:T(8,128)(2,1)}), bf16[4,256,1,256]{1,3,2,0:T(8,128)(2,1)S(1)}, u32[]{:S(2)}, u32[]{:S(2)}) async-start(bf16[4,256,1,256]{1,3,2,0:T(8,128)(2,1)} %broadcast_in_dim.32), calls=%async_computation.7 | async-start | bytes 1048576 | tf_op jit(solution)/shard_map/all_to_all | solution.py:11
  160.4 1.7 fusion.21
  162.1 19.1 %all-to-all-done.7 = bf16[4,256,1,256]{1,3,2,0:T(8,128)(2,1)S(1)} async-done(((bf16[4,256,1,256]{1,3,2,0:T(8,128)(2,1)}), bf16[4,256,1,256]{1,3,2,0:T(8,128)(2,1)S(1)}, u32[]{:S(2)}, u32[]{:S(2)}) %all-to-all-start.7) | async-done | bytes 524320 | tf_op jit(solution)/shard_map/all_to_all | solution.py:11
  181.2 3.7 %fusion.24 = bf16[256,1024]{1,0:T(8,128)(2,1)S(1)} fusion(bf16[1,1024,1024]{2,1,0:T(8,128)(2,1)S(1)} %copy-done, bf16[256,1024]{0,1:T(8,128)(2,1)S(1)} %bitcast.139, bf16[1,1024,1024]{2,1,0:T(8,128)(2,1)} %param.11, f32[256,1,1024]{2,0,1:T(8,128)} %fusion.21), kind=kOutput, calls=%fused_computation.16 | convolution fusion | flops 1078984704 | bytes 6291456 | tf_op jit(solution)/shard_map/ref,ekf->rek/dot_general | solution.py:113
  185.8 8.2 %all-to-all-start.8 = ((bf16[4,256,1,256]{3,1,2,0:T(8,128)(2,1)}), bf16[4,256,1,256]{3,1,2,0:T(8,128)(2,1)S(1)}, u32[]{:S(2)}, u32[]{:S(2)}) async-start(bf16[4,256,1,256]{3,1,2,0:T(8,128)(2,1)} %bitcast.134), calls=%async_computation.8 | async-start | bytes 1048576 | tf_op jit(solution)/shard_map/all_to_all | solution.py:37
  194.0 2.7 fusion.27
  197.6 18.0 %all-to-all-done.8 = bf16[4,256,1,256]{3,1,2,0:T(8,128)(2,1)S(1)} async-done(((bf16[4,256,1,256]{3,1,2,0:T(8,128)(2,1)}), bf16[4,256,1,256]{3,1,2,0:T(8,128)(2,1)S(1)}, u32[]{:S(2)}, u32[]{:S(2)}) %all-to-all-start.8) | async-done | bytes 524320 | tf_op jit(solution)/shard_map/all_to_all | solution.py:37
  215.6 4.1 %all-to-all-start.3 = ((bf16[4,256,1,256]{3,1,2,0:T(8,128)(2,1)}), bf16[4,256,1,256]{3,1,2,0:T(8,128)(2,1)S(1)}, u32[]{:S(2)}, u32[]{:S(2)}) async-start(bf16[4,256,1,256]{3,1,2,0:T(8,128)(2,1)} %bitcast.138), calls=%async_computation.3 | async-start | bytes 1048576 | tf_op jit(solution)/shard_map/all_to_all | solution.py:37
  220.4 1.6 reshape.121
  222.0 18.7 %all-to-all-done.3 = bf16[4,256,1,256]{3,1,2,0:T(8,128)(2,1)S(1)} async-done(((bf16[4,256,1,256]{3,1,2,0:T(8,128)(2,1)}), bf16[4,256,1,256]{3,1,2,0:T(8,128)(2,1)S(1)}, u32[]{:S(2)}, u32[]{:S(2)}) %all-to-all-start.3) | async-done | bytes 524320 | tf_op jit(solution)/shard_map/all_to_all | solution.py:37
  240.8 18.6 %all-to-all-start.9 = ((bf16[128,2,1,256]{3,1,2,0:T(2,128)(2,1)}), bf16[128,2,1,256]{3,1,2,0:T(2,128)(2,1)}, u32[]{:S(2)}, u32[]{:S(2)}) async-start(bf16[128,2,1,256]{3,1,2,0:T(2,128)(2,1)} %bitcast.37), calls=%async_computation.9 | async-start | bytes 262144 | tf_op jit(solution)/shard_map/all_to_all | solution.py:115
  259.4 1.2 convert_element_type.119
  262.4 9.7 %all-to-all-done.9 = bf16[128,2,1,256]{3,1,2,0:T(2,128)(2,1)} async-done(((bf16[128,2,1,256]{3,1,2,0:T(2,128)(2,1)}), bf16[128,2,1,256]{3,1,2,0:T(2,128)(2,1)}, u32[]{:S(2)}, u32[]{:S(2)}) %all-to-all-start.9) | async-done | bytes 131104 | tf_op jit(solution)/shard_map/all_to_all | solution.py:115
  272.1 10.3 %all-to-all-start.4 = ((bf16[128,2,1,256]{3,1,2,0:T(2,128)(2,1)}), bf16[128,2,1,256]{3,1,2,0:T(2,128)(2,1)S(1)}, u32[]{:S(2)}, u32[]{:S(2)}) async-start(bf16[128,2,1,256]{3,1,2,0:T(2,128)(2,1)} %copy.119), calls=%async_computation.4 | async-start | bytes 262144 | tf_op jit(solution)/shard_map/all_to_all | solution.py:88
  282.3 1.2 fusion.43
  283.6 10.4 %all-to-all-done.4 = bf16[128,2,1,256]{3,1,2,0:T(2,128)(2,1)S(1)} async-done(((bf16[128,2,1,256]{3,1,2,0:T(2,128)(2,1)}), bf16[128,2,1,256]{3,1,2,0:T(2,128)(2,1)S(1)}, u32[]{:S(2)}, u32[]{:S(2)}) %all-to-all-start.4) | async-done | bytes 131104 | tf_op jit(solution)/shard_map/all_to_all | solution.py:88
  295.0 9.0 %all-to-all-start.10 = ((bf16[4,2,196,128]{3,1,2,0:T(2,128)(2,1)}), bf16[4,2,196,128]{3,1,2,0:T(2,128)(2,1)S(1)}, u32[]{:S(2)}, u32[]{:S(2)}) async-start(bf16[4,2,196,128]{3,1,2,0:T(2,128)(2,1)} %broadcast_in_dim.33), calls=%async_computation.10 | async-start | bytes 802816 | tf_op jit(solution)/shard_map/all_to_all | solution.py:11
  304.3 28.1 %all-to-all-done.10 = bf16[4,2,196,128]{3,1,2,0:T(2,128)(2,1)S(1)} async-done(((bf16[4,2,196,128]{3,1,2,0:T(2,128)(2,1)}), bf16[4,2,196,128]{3,1,2,0:T(2,128)(2,1)S(1)}, u32[]{:S(2)}, u32[]{:S(2)}) %all-to-all-start.10) | async-done | bytes 401440 | tf_op jit(solution)/shard_map/all_to_all | solution.py:11
  333.4 4.0 %all-to-all-start.5 = ((bf16[4,2,196,128]{3,1,2,0:T(2,128)(2,1)}), bf16[4,2,196,128]{3,1,2,0:T(2,128)(2,1)S(1)}, u32[]{:S(2)}, u32[]{:S(2)}) async-start(bf16[4,2,196,128]{3,1,2,0:T(2,128)(2,1)} %broadcast_in_dim.14), calls=%async_computation.5 | async-start | bytes 802816 | tf_op jit(solution)/shard_map/all_to_all | solution.py:11
  340.2 1.2 multiply_reduce_fusion
  341.3 16.2 %all-to-all-done.5 = bf16[4,2,196,128]{3,1,2,0:T(2,128)(2,1)S(1)} async-done(((bf16[4,2,196,128]{3,1,2,0:T(2,128)(2,1)}), bf16[4,2,196,128]{3,1,2,0:T(2,128)(2,1)S(1)}, u32[]{:S(2)}, u32[]{:S(2)}) %all-to-all-start.5) | async-done | bytes 401440 | tf_op jit(solution)/shard_map/all_to_all | solution.py:11
  357.9 3.9 %fusion.41 = bf16[2,196,128]{2,0,1:T(2,128)(2,1)S(1)} fusion(f32[2,196,128]{2,0,1:T(2,128)} %get-tuple-element.27, f32[2,196,128]{2,0,1:T(2,128)S(1)} %convert_reduce_fusion.2, f32[2,196,128]{2,0,1:T(2,128)} %get-tuple-element.33, f32[2,196,128]{2,0,1:T(2,128)S(1)} %convert_reduce_fusion.1, f32[2,128]{1,0:T(2,128)S(1)} %multiply_reduce_fusion, ...), kind=kOutput, calls=%fused_computation.31 | output fusion | flops 401927 | bytes 905760 | tf_op jit(solution)/shard_map/sub | solution.py:129
  (47 shorter events, 18.1 us)
Async XLA Ops:
  0.6 159.8 %copy-start = (bf16[1,1024,1024]{2,1,0:T(8,128)(2,1)S(1)}, bf16[1,1024,1024]{2,1,0:T(8,128)(2,1)}, u32[]{:S(2)}) copy-start(bf16[1,1024,1024]{2,1,0:T(8,128)(2,1)} %param.9) | copy-start | bytes 6291460
  63.2 15.9 %copy-start.2 = (bf16[2,196,256]{2,0,1:T(2,128)(2,1)S(1)}, bf16[2,196,256]{2,0,1:T(2,128)(2,1)}, u32[]{:S(2)}) copy-start(bf16[2,196,256]{2,0,1:T(2,128)(2,1)} %param.13) | copy-start | bytes 602116
  67.6 23.2 %all-to-all-start.1 = ((bf16[2,128,256]{2,0,1:T(2,128)(2,1)}), bf16[2,128,256]{2,0,1:T(2,128)(2,1)S(1)}, u32[]{:S(2)}, u32[]{:S(2)}) async-start(bf16[2,128,256]{2,0,1:T(2,128)(2,1)} %copy.114), calls=%async_computation.1 | async-start | bytes 262144 | tf_op jit(solution)/shard_map/all_to_all | solution.py:75
  90.8 23.3 %all-to-all-start.6 = ((bf16[2,128,256]{2,0,1:T(2,128)(2,1)}), bf16[2,128,256]{2,0,1:T(2,128)(2,1)S(1)}, u32[]{:S(2)}, u32[]{:S(2)}) async-start(bf16[2,128,256]{2,0,1:T(2,128)(2,1)} %copy.126), calls=%async_computation.6 | async-start | bytes 262144 | tf_op jit(solution)/shard_map/all_to_all | solution.py:105
  114.9 39.9 %all-to-all-start.2 = ((bf16[4,256,1,256]{1,3,2,0:T(8,128)(2,1)}), bf16[4,256,1,256]{1,3,2,0:T(8,128)(2,1)S(1)}, u32[]{:S(2)}, u32[]{:S(2)}) async-start(bf16[4,256,1,256]{1,3,2,0:T(8,128)(2,1)} %broadcast_in_dim.13), calls=%async_computation.2 | async-start | bytes 1048576 | tf_op jit(solution)/shard_map/all_to_all | solution.py:11
  155.7 25.6 %all-to-all-start.7 = ((bf16[4,256,1,256]{1,3,2,0:T(8,128)(2,1)}), bf16[4,256,1,256]{1,3,2,0:T(8,128)(2,1)S(1)}, u32[]{:S(2)}, u32[]{:S(2)}) async-start(bf16[4,256,1,256]{1,3,2,0:T(8,128)(2,1)} %broadcast_in_dim.32), calls=%async_computation.7 | async-start | bytes 1048576 | tf_op jit(solution)/shard_map/all_to_all | solution.py:11
  185.8 29.8 %all-to-all-start.8 = ((bf16[4,256,1,256]{3,1,2,0:T(8,128)(2,1)}), bf16[4,256,1,256]{3,1,2,0:T(8,128)(2,1)S(1)}, u32[]{:S(2)}, u32[]{:S(2)}) async-start(bf16[4,256,1,256]{3,1,2,0:T(8,128)(2,1)} %bitcast.134), calls=%async_computation.8 | async-start | bytes 1048576 | tf_op jit(solution)/shard_map/all_to_all | solution.py:37
  215.6 25.2 %all-to-all-start.3 = ((bf16[4,256,1,256]{3,1,2,0:T(8,128)(2,1)}), bf16[4,256,1,256]{3,1,2,0:T(8,128)(2,1)S(1)}, u32[]{:S(2)}, u32[]{:S(2)}) async-start(bf16[4,256,1,256]{3,1,2,0:T(8,128)(2,1)} %bitcast.138), calls=%async_computation.3 | async-start | bytes 1048576 | tf_op jit(solution)/shard_map/all_to_all | solution.py:37
  240.8 31.3 %all-to-all-start.9 = ((bf16[128,2,1,256]{3,1,2,0:T(2,128)(2,1)}), bf16[128,2,1,256]{3,1,2,0:T(2,128)(2,1)}, u32[]{:S(2)}, u32[]{:S(2)}) async-start(bf16[128,2,1,256]{3,1,2,0:T(2,128)(2,1)} %bitcast.37), calls=%async_computation.9 | async-start | bytes 262144 | tf_op jit(solution)/shard_map/all_to_all | solution.py:115
  260.7 43.2 %copy-start.3 = (bf16[2,196,256]{2,0,1:T(2,128)(2,1)S(1)}, bf16[2,196,256]{2,0,1:T(2,128)(2,1)}, u32[]{:S(2)}) copy-start(bf16[2,196,256]{2,0,1:T(2,128)(2,1)} %param.13) | copy-start | bytes 602116
  272.1 22.0 %all-to-all-start.4 = ((bf16[128,2,1,256]{3,1,2,0:T(2,128)(2,1)}), bf16[128,2,1,256]{3,1,2,0:T(2,128)(2,1)S(1)}, u32[]{:S(2)}, u32[]{:S(2)}) async-start(bf16[128,2,1,256]{3,1,2,0:T(2,128)(2,1)} %copy.119), calls=%async_computation.4 | async-start | bytes 262144 | tf_op jit(solution)/shard_map/all_to_all | solution.py:88
  295.0 37.4 %all-to-all-start.10 = ((bf16[4,2,196,128]{3,1,2,0:T(2,128)(2,1)}), bf16[4,2,196,128]{3,1,2,0:T(2,128)(2,1)S(1)}, u32[]{:S(2)}, u32[]{:S(2)}) async-start(bf16[4,2,196,128]{3,1,2,0:T(2,128)(2,1)} %broadcast_in_dim.33), calls=%async_computation.10 | async-start | bytes 802816 | tf_op jit(solution)/shard_map/all_to_all | solution.py:11
  333.4 24.1 %all-to-all-start.5 = ((bf16[4,2,196,128]{3,1,2,0:T(2,128)(2,1)}), bf16[4,2,196,128]{3,1,2,0:T(2,128)(2,1)S(1)}, u32[]{:S(2)}, u32[]{:S(2)}) async-start(bf16[4,2,196,128]{3,1,2,0:T(2,128)(2,1)} %broadcast_in_dim.14), calls=%async_computation.5 | async-start | bytes 802816 | tf_op jit(solution)/shard_map/all_to_all | solution.py:11
  338.1 19.8 %copy-start.4 = (f32[2,196]{0,1:T(8,128)S(1)}, f32[2,196]{0,1:T(8,128)}, u32[]{:S(2)}) copy-start(f32[2,196]{0,1:T(8,128)} %get-tuple-element.31) | copy-start | bytes 4708
  339.8 22.0 %copy-start.1 = (bf16[256,128]{1,0:T(8,128)(2,1)S(1)}, bf16[256,128]{1,0:T(8,128)(2,1)}, u32[]{:S(2)}) copy-start(bf16[256,128]{1,0:T(8,128)(2,1)} %param.8) | copy-start | bytes 196612
where the time goes:
time: 365 us; the launch traced here: 364 us
  waiting for transfers between devices  176 us (48%)
  starting transfers between devices  87.7 us (24%)
  blocking collectives  60.5 us (17%)
  matrix products  13.7 us (4%)
  other arithmetic  12.8 us (4%)
  local copies, waits for them, and re-layouts  12.5 us (3%)
    all_to_all x4, waiting for transfers between devices, sent_to_all(): return lax.all_to_all(copies, axis, split_axis=0, concat_axis=0, tiled=True)  96.9 us
    all_to_all x1, blocking collectives, sent_to_all(): return lax.all_to_all(copies, axis, split_axis=0, concat_axis=0, tiled=True)  60.5 us
    all_to_all x2, waiting for transfers between devices, sent_and_summed(): tiles = lax.all_to_all(split_up(x, dim, peers), axis, 0, 0, tiled=True)  36.8 us
    all_to_all x4, starting transfers between devices, sent_to_all(): return lax.all_to_all(copies, axis, split_axis=0, concat_axis=0, tiled=True)  23.4 us
    all_to_all x1, starting transfers between devices, per_device(): lax.all_to_all(slot_grad.reshape(groups, images_dev, local_experts, quart...  18.6 us
    all_to_all x2, starting transfers between devices, sent_and_summed(): tiles = lax.all_to_all(split_up(x, dim, peers), axis, 0, 0, tiled=True)  12.3 us
    all_to_all x1, starting transfers between devices, per_device(): lax.all_to_all(out_grad, 'expert', split_axis=1, concat_axis=0, tiled=True)  11.6 us
    all_to_all x1, starting transfers between devices, per_device(): lax.all_to_all(slot_in, 'expert', split_axis=1, concat_axis=0, tiled=True)  11.5 us
  transfers between devices with their start and end apart: 10, of which 10 were waited for; matrix products, arithmetic and copies ran while one was open for 5% of the time, Pallas kernels for 0%

commit v1 on v0

--- a/solution.py
+++ b/solution.py
@@ -102,7 +102,12 @@
     out_grad = jnp.einsum(
         "its,itd->isd", combine_low, cotangent, preferred_element_type=jnp.float32
     ).astype(jnp.bfloat16)
-    grad_arrived = lax.all_to_all(out_grad, "expert", split_axis=1, concat_axis=0, tiled=True)
+    grad_arrived = jnp.concatenate(
+        lax.all_to_all(
+            jnp.stack(jnp.split(out_grad, lax.axis_size("expert"), axis=1)), "expert", 0, 0
+        ),
+        axis=0,
+    )
     hidden_grad = jnp.einsum(
         "ren,efn->ref",
         gathered_copies(grad_arrived, "hidden", 2),

time: 365 us -> 433 us (1.19)
  local copies, waits for them, and re-layouts: 12.5 us -> 89.5 us
  waiting for transfers between devices: 176 us -> 160 us
  starting transfers between devices: 87.7 us -> 95.3 us
    unnamed x13 -> x144, local copies, waits for them, and re-layouts: 2.36 us -> 76.2 us
    all_to_all x1, waiting for transfers between devices: 10.7 us -> 0.01 us  [per_device(): lax.all_to_all(slot_in, 'expert', split_axis=1, concat_axis=0, tiled=True)]
    all_to_all x2, waiting for transfers between devices: 36.8 us -> 29.9 us  [sent_and_summed(): tiles = lax.all_to_all(split_up(x, dim, peers), axis, 0, 0, tiled=True)]
    all_to_all x1, starting transfers between devices: 18.6 us -> 23.2 us  [per_device(): lax.all_to_all(slot_grad.reshape(groups, images_dev, local_experts, quart...]
    all_to_all x1, starting transfers between devices: 11.6 us -> 16 us  [per_device(): lax.all_to_all(jnp.stack(jnp.split(out_grad, lax.axis_size('expert'), axi...]
  transfers between devices with their start and end apart: 10 -> 10, of which waited for: 10 -> 9; matrix products, arithmetic and copies ran while one was open for 5% -> 21% of each run, Pallas kernels for 0% -> 0%
where the time goes in v1:
time: 433 us; the launch traced here: 432 us
  waiting for transfers between devices  160 us (37%)
  starting transfers between devices  95.3 us (22%)
  local copies, waits for them, and re-layouts  89.5 us (21%)
  blocking collectives  60.5 us (14%)
  matrix products  15.3 us (4%)
  other arithmetic  10.5 us (2%)
    all_to_all x4, waiting for transfers between devices, sent_to_all(): return lax.all_to_all(copies, axis, split_axis=0, concat_axis=0, tiled=True)  96.8 us
    unnamed x144, local copies, waits for them, and re-layouts  76.2 us
    all_to_all x1, blocking collectives, sent_to_all(): return lax.all_to_all(copies, axis, split_axis=0, concat_axis=0, tiled=True)  60.5 us
    all_to_all x2, waiting for transfers between devices, sent_and_summed(): tiles = lax.all_to_all(split_up(x, dim, peers), axis, 0, 0, tiled=True)  29.9 us
    all_to_all x1, starting transfers between devices, per_device(): lax.all_to_all(slot_grad.reshape(groups, images_dev, local_experts, quart...  23.2 us
    all_to_all x4, starting transfers between devices, sent_to_all(): return lax.all_to_all(copies, axis, split_axis=0, concat_axis=0, tiled=True)  22 us
    all_to_all x1, starting transfers between devices, per_device(): lax.all_to_all(jnp.stack(jnp.split(out_grad, lax.axis_size('expert'), axi...  16 us
    all_to_all x2, starting transfers between devices, sent_and_summed(): tiles = lax.all_to_all(split_up(x, dim, peers), axis, 0, 0, tiled=True)  12.2 us
  transfers between devices with their start and end apart: 10, of which 9 were waited for; matrix products, arithmetic and copies ran while one was open for 21% of the time, Pallas kernels for 0%

profile of v1, /device:TPU:49, one launch (start us, length us, event | category | flops | bytes accessed | tf_op | source)
XLA Modules:
  0.0 432.1 jit_solution(6445667042676074697)
XLA Ops:
  0.6 1.3 fusion.72
  2.3 60.5 %all_to_all.88 = f32[4,2,196,128]{3,1,2,0:T(2,128)S(1)} all-to-all(f32[4,2,196,128]{3,1,2,0:T(2,128)S(1)} %broadcast_in_dim.12), channel_id=1, replica_groups=mesh['expert'=128,'hidden'=4] {'hidden'}, dimensions={0} | all-to-all | bytes 1605632 | tf_op jit(solution)/shard_map/all_to_all | solution.py:11
  63.5 1.4 exponential_reduce_fusion
  69.1 11.5 %all-to-all-start.1 = ((bf16[2,128,256]{2,0,1:T(2,128)(2,1)}), bf16[2,128,256]{2,0,1:T(2,128)(2,1)S(1)}, u32[]{:S(2)}, u32[]{:S(2)}) async-start(bf16[2,128,256]{2,0,1:T(2,128)(2,1)} %copy.3948), calls=%async_computation.1 | async-start | bytes 262144 | tf_op jit(solution)/shard_map/all_to_all | solution.py:75
  153.7 16.0 %all-to-all-start.6 = ((bf16[128,2,1,256]{3,1,2,0:T(2,128)(2,1)}), bf16[128,2,1,256]{3,1,2,0:T(2,128)(2,1)S(1)}, u32[]{:S(2)}, u32[]{:S(2)}) async-start(bf16[128,2,1,256]{3,1,2,0:T(2,128)(2,1)} %constant_dynamic-update-slice_fusion), calls=%async_computation.6 | async-start | bytes 262144 | tf_op jit(solution)/shard_map/all_to_all | solution.py:106
  170.0 11.3 %all-to-all-done.6 = bf16[128,2,1,256]{3,1,2,0:T(2,128)(2,1)S(1)} async-done(((bf16[128,2,1,256]{3,1,2,0:T(2,128)(2,1)}), bf16[128,2,1,256]{3,1,2,0:T(2,128)(2,1)S(1)}, u32[]{:S(2)}, u32[]{:S(2)}) %all-to-all-start.6) | async-done | bytes 131104 | tf_op jit(solution)/shard_map/all_to_all | solution.py:106
  182.1 6.4 %all-to-all-start.2 = ((bf16[4,256,1,256]{1,3,2,0:T(8,128)(2,1)}), bf16[4,256,1,256]{1,3,2,0:T(8,128)(2,1)S(1)}, u32[]{:S(2)}, u32[]{:S(2)}) async-start(bf16[4,256,1,256]{1,3,2,0:T(8,128)(2,1)} %broadcast_in_dim.13), calls=%async_computation.2 | async-start | bytes 1048576 | tf_op jit(solution)/shard_map/all_to_all | solution.py:11
  188.7 33.4 %all-to-all-done.2 = bf16[4,256,1,256]{1,3,2,0:T(8,128)(2,1)S(1)} async-done(((bf16[4,256,1,256]{1,3,2,0:T(8,128)(2,1)}), bf16[4,256,1,256]{1,3,2,0:T(8,128)(2,1)S(1)}, u32[]{:S(2)}, u32[]{:S(2)}) %all-to-all-start.2) | async-done | bytes 524320 | tf_op jit(solution)/shard_map/all_to_all | solution.py:11
  223.0 4.0 all-to-all-start.7
  227.0 1.7 fusion.21
  228.7 19.8 %all-to-all-done.7 = bf16[4,256,1,256]{1,3,2,0:T(8,128)(2,1)S(1)} async-done(((bf16[4,256,1,256]{1,3,2,0:T(8,128)(2,1)}), bf16[4,256,1,256]{1,3,2,0:T(8,128)(2,1)S(1)}, u32[]{:S(2)}, u32[]{:S(2)}) %all-to-all-start.7) | async-done | bytes 524320 | tf_op jit(solution)/shard_map/all_to_all | solution.py:11
  248.6 4.5 %fusion.39 = bf16[256,1,1024]{2,0,1:T(8,128)(2,1)} fusion(bf16[1,1024,1024]{2,1,0:T(8,128)(2,1)S(1)} %copy-done, bf16[256,1024]{0,1:T(8,128)(2,1)S(1)} %bitcast.393, bf16[1,1024,1024]{2,1,0:T(8,128)(2,1)} %param.11, f32[256,1,1024]{2,0,1:T(8,128)} %fusion.21), kind=kOutput, calls=%fused_computation.21 | convolution fusion | flops 1078984704 | bytes 6291456 | tf_op jit(solution)/shard_map/ref,ekf->rek/dot_general | solution.py:118
  253.1 1.4 reshape.124
  255.4 8.2 %all-to-all-start.8 = ((bf16[4,256,1,256]{3,1,2,0:T(8,128)(2,1)}), bf16[4,256,1,256]{3,1,2,0:T(8,128)(2,1)S(1)}, u32[]{:S(2)}, u32[]{:S(2)}) async-start(bf16[4,256,1,256]{3,1,2,0:T(8,128)(2,1)} %copy.3964), calls=%async_computation.8 | async-start | bytes 1048576 | tf_op jit(solution)/shard_map/all_to_all | solution.py:37
  263.5 3.5 fusion.36
  267.1 1.4 reshape.119
  269.4 15.7 %all-to-all-done.8 = bf16[4,256,1,256]{3,1,2,0:T(8,128)(2,1)S(1)} async-done(((bf16[4,256,1,256]{3,1,2,0:T(8,128)(2,1)}), bf16[4,256,1,256]{3,1,2,0:T(8,128)(2,1)S(1)}, u32[]{:S(2)}, u32[]{:S(2)}) %all-to-all-start.8) | async-done | bytes 524320 | tf_op jit(solution)/shard_map/all_to_all | solution.py:37
  285.1 4.1 all-to-all-start.3
  289.9 1.6 reshape.125
  291.5 14.2 %all-to-all-done.3 = bf16[4,256,1,256]{3,1,2,0:T(8,128)(2,1)S(1)} async-done(((bf16[4,256,1,256]{3,1,2,0:T(8,128)(2,1)}), bf16[4,256,1,256]{3,1,2,0:T(8,128)(2,1)S(1)}, u32[]{:S(2)}, u32[]{:S(2)}) %all-to-all-start.3) | async-done | bytes 524320 | tf_op jit(solution)/shard_map/all_to_all | solution.py:37
  305.7 23.2 %all-to-all-start.9 = ((bf16[128,2,1,256]{3,1,2,0:T(2,128)(2,1)}), bf16[128,2,1,256]{3,1,2,0:T(2,128)(2,1)}, u32[]{:S(2)}, u32[]{:S(2)}) async-start(bf16[128,2,1,256]{3,1,2,0:T(2,128)(2,1)} %bitcast.35), calls=%async_computation.9 | async-start | bytes 262144 | tf_op jit(solution)/shard_map/all_to_all | solution.py:120
  330.0 11.5 %all-to-all-done.9 = bf16[128,2,1,256]{3,1,2,0:T(2,128)(2,1)} async-done(((bf16[128,2,1,256]{3,1,2,0:T(2,128)(2,1)}), bf16[128,2,1,256]{3,1,2,0:T(2,128)(2,1)}, u32[]{:S(2)}, u32[]{:S(2)}) %all-to-all-start.9) | async-done | bytes 131104 | tf_op jit(solution)/shard_map/all_to_all | solution.py:120
  341.5 10.3 %all-to-all-start.4 = ((bf16[128,2,1,256]{3,1,2,0:T(2,128)(2,1)}), bf16[128,2,1,256]{3,1,2,0:T(2,128)(2,1)S(1)}, u32[]{:S(2)}, u32[]{:S(2)}) async-start(bf16[128,2,1,256]{3,1,2,0:T(2,128)(2,1)} %copy.3955), calls=%async_computation.4 | async-start | bytes 262144 | tf_op jit(solution)/shard_map/all_to_all | solution.py:88
  351.8 1.2 fusion.49
  353.1 10.4 %all-to-all-done.4 = bf16[128,2,1,256]{3,1,2,0:T(2,128)(2,1)S(1)} async-done(((bf16[128,2,1,256]{3,1,2,0:T(2,128)(2,1)}), bf16[128,2,1,256]{3,1,2,0:T(2,128)(2,1)S(1)}, u32[]{:S(2)}, u32[]{:S(2)}) %all-to-all-start.4) | async-done | bytes 131104 | tf_op jit(solution)/shard_map/all_to_all | solution.py:88
  364.5 7.6 %all-to-all-start.10 = ((bf16[4,2,196,128]{3,1,2,0:T(2,128)(2,1)}), bf16[4,2,196,128]{3,1,2,0:T(2,128)(2,1)S(1)}, u32[]{:S(2)}, u32[]{:S(2)}) async-start(bf16[4,2,196,128]{3,1,2,0:T(2,128)(2,1)} %broadcast_in_dim.33), calls=%async_computation.10 | async-start | bytes 802816 | tf_op jit(solution)/shard_map/all_to_all | solution.py:11
  372.4 28.2 %all-to-all-done.10 = bf16[4,2,196,128]{3,1,2,0:T(2,128)(2,1)S(1)} async-done(((bf16[4,2,196,128]{3,1,2,0:T(2,128)(2,1)}), bf16[4,2,196,128]{3,1,2,0:T(2,128)(2,1)S(1)}, u32[]{:S(2)}, u32[]{:S(2)}) %all-to-all-start.10) | async-done | bytes 401440 | tf_op jit(solution)/shard_map/all_to_all | solution.py:11
  401.5 4.0 all-to-all-start.5
  405.5 1.6 multiply_multiply_fusion.1
  407.1 1.6 copy.3973
  410.3 15.4 %all-to-all-done.5 = bf16[4,2,196,128]{3,1,2,0:T(2,128)(2,1)S(1)} async-done(((bf16[4,2,196,128]{3,1,2,0:T(2,128)(2,1)}), bf16[4,2,196,128]{3,1,2,0:T(2,128)(2,1)S(1)}, u32[]{:S(2)}, u32[]{:S(2)}) %all-to-all-start.5) | async-done | bytes 401440 | tf_op jit(solution)/shard_map/all_to_all | solution.py:11
  426.1 3.8 fusion.47
  (189 shorter events, 90.3 us)
Async XLA Ops:
  0.6 226.4 %copy-start = (bf16[1,1024,1024]{2,1,0:T(8,128)(2,1)S(1)}, bf16[1,1024,1024]{2,1,0:T(8,128)(2,1)}, u32[]{:S(2)}) copy-start(bf16[1,1024,1024]{2,1,0:T(8,128)(2,1)} %param.9) | copy-start | bytes 6291460
  63.2 4.9 %copy-start.1 = (bf16[2,196,256]{2,0,1:T(2,128)(2,1)S(1)}, bf16[2,196,256]{2,0,1:T(2,128)(2,1)}, u32[]{:S(2)}) copy-start(bf16[2,196,256]{2,0,1:T(2,128)(2,1)} %param.7) | copy-start | bytes 602116
  69.1 84.5 %all-to-all-start.1 = ((bf16[2,128,256]{2,0,1:T(2,128)(2,1)}), bf16[2,128,256]{2,0,1:T(2,128)(2,1)S(1)}, u32[]{:S(2)}, u32[]{:S(2)}) async-start(bf16[2,128,256]{2,0,1:T(2,128)(2,1)} %copy.3948), calls=%async_computation.1 | async-start | bytes 262144 | tf_op jit(solution)/shard_map/all_to_all | solution.py:75
  153.7 27.6 %all-to-all-start.6 = ((bf16[128,2,1,256]{3,1,2,0:T(2,128)(2,1)}), bf16[128,2,1,256]{3,1,2,0:T(2,128)(2,1)S(1)}, u32[]{:S(2)}, u32[]{:S(2)}) async-start(bf16[128,2,1,256]{3,1,2,0:T(2,128)(2,1)} %constant_dynamic-update-slice_fusion), calls=%async_computation.6 | async-start | bytes 262144 | tf_op jit(solution)/shard_map/all_to_all | solution.py:106
  169.9 57.1 %copy-start.5 = (bf16[1,1024]{1,0:T(2,128)(2,1)S(1)}, bf16[1,1024]{1,0:T(2,128)(2,1)}, u32[]{:S(2)}) copy-start(bf16[1,1024]{1,0:T(2,128)(2,1)} %param.10) | copy-start | bytes 6148
  182.1 40.0 %all-to-all-start.2 = ((bf16[4,256,1,256]{1,3,2,0:T(8,128)(2,1)}), bf16[4,256,1,256]{1,3,2,0:T(8,128)(2,1)S(1)}, u32[]{:S(2)}, u32[]{:S(2)}) async-start(bf16[4,256,1,256]{1,3,2,0:T(8,128)(2,1)} %broadcast_in_dim.13), calls=%async_computation.2 | async-start | bytes 1048576 | tf_op jit(solution)/shard_map/all_to_all | solution.py:11
  223.0 25.6 %all-to-all-start.7 = ((bf16[4,256,1,256]{1,3,2,0:T(8,128)(2,1)}), bf16[4,256,1,256]{1,3,2,0:T(8,128)(2,1)S(1)}, u32[]{:S(2)}, u32[]{:S(2)}) async-start(bf16[4,256,1,256]{1,3,2,0:T(8,128)(2,1)} %broadcast_in_dim.32), calls=%async_computation.7 | async-start | bytes 1048576 | tf_op jit(solution)/shard_map/all_to_all | solution.py:11
  255.4 29.7 %all-to-all-start.8 = ((bf16[4,256,1,256]{3,1,2,0:T(8,128)(2,1)}), bf16[4,256,1,256]{3,1,2,0:T(8,128)(2,1)S(1)}, u32[]{:S(2)}, u32[]{:S(2)}) async-start(bf16[4,256,1,256]{3,1,2,0:T(8,128)(2,1)} %copy.3964), calls=%async_computation.8 | async-start | bytes 1048576 | tf_op jit(solution)/shard_map/all_to_all | solution.py:37
  267.1 61.9 %copy-start.6 = (bf16[1,256]{1,0:T(2,128)(2,1)S(1)}, bf16[1,256]{1,0:T(2,128)(2,1)}, u32[]{:S(2)}) copy-start(bf16[1,256]{1,0:T(2,128)(2,1)} %param.12) | copy-start | bytes 1540
  285.1 20.6 %all-to-all-start.3 = ((bf16[4,256,1,256]{3,1,2,0:T(8,128)(2,1)}), bf16[4,256,1,256]{3,1,2,0:T(8,128)(2,1)S(1)}, u32[]{:S(2)}, u32[]{:S(2)}) async-start(bf16[4,256,1,256]{3,1,2,0:T(8,128)(2,1)} %copy.3953), calls=%async_computation.3 | async-start | bytes 1048576 | tf_op jit(solution)/shard_map/all_to_all | solution.py:37
  305.7 35.8 %all-to-all-start.9 = ((bf16[128,2,1,256]{3,1,2,0:T(2,128)(2,1)}), bf16[128,2,1,256]{3,1,2,0:T(2,128)(2,1)}, u32[]{:S(2)}, u32[]{:S(2)}) async-start(bf16[128,2,1,256]{3,1,2,0:T(2,128)(2,1)} %bitcast.35), calls=%async_computation.9 | async-start | bytes 262144 | tf_op jit(solution)/shard_map/all_to_all | solution.py:120
  329.0 43.0 %copy-start.4 = (bf16[2,196,256]{2,0,1:T(2,128)(2,1)S(1)}, bf16[2,196,256]{2,0,1:T(2,128)(2,1)}, u32[]{:S(2)}) copy-start(bf16[2,196,256]{2,0,1:T(2,128)(2,1)} %param.13) | copy-start | bytes 602116
  341.5 22.0 %all-to-all-start.4 = ((bf16[128,2,1,256]{3,1,2,0:T(2,128)(2,1)}), bf16[128,2,1,256]{3,1,2,0:T(2,128)(2,1)S(1)}, u32[]{:S(2)}, u32[]{:S(2)}) async-start(bf16[128,2,1,256]{3,1,2,0:T(2,128)(2,1)} %copy.3955), calls=%async_computation.4 | async-start | bytes 262144 | tf_op jit(solution)/shard_map/all_to_all | solution.py:88
  364.5 36.0 %all-to-all-start.10 = ((bf16[4,2,196,128]{3,1,2,0:T(2,128)(2,1)}), bf16[4,2,196,128]{3,1,2,0:T(2,128)(2,1)S(1)}, u32[]{:S(2)}, u32[]{:S(2)}) async-start(bf16[4,2,196,128]{3,1,2,0:T(2,128)(2,1)} %broadcast_in_dim.33), calls=%async_computation.10 | async-start | bytes 802816 | tf_op jit(solution)/shard_map/all_to_all | solution.py:11
  372.1 38.0 %copy-start.2 = (f32[2,196,128]{2,0,1:T(2,128)S(1)}, f32[2,196,128]{2,0,1:T(2,128)}, u32[]{:S(2)}) copy-start(f32[2,196,128]{2,0,1:T(2,128)} %get-tuple-element.123) | copy-start | bytes 602116
  401.5 24.2 %all-to-all-start.5 = ((bf16[4,2,196,128]{3,1,2,0:T(2,128)(2,1)}), bf16[4,2,196,128]{3,1,2,0:T(2,128)(2,1)S(1)}, u32[]{:S(2)}, u32[]{:S(2)}) async-start(bf16[4,2,196,128]{3,1,2,0:T(2,128)(2,1)} %broadcast_in_dim.14), calls=%async_computation.5 | async-start | bytes 802816 | tf_op jit(solution)/shard_map/all_to_all | solution.py:11
  409.7 20.2 %copy-start.3 = (bf16[256,128]{1,0:T(8,128)(2,1)S(1)}, bf16[256,128]{1,0:T(8,128)(2,1)}, u32[]{:S(2)}) copy-start(bf16[256,128]{1,0:T(8,128)(2,1)} %param.8) | copy-start | bytes 196612
